TPU v7x, 128 devices: a whole 4x4x4 slice. The times are simulated.
128 devices in a mesh: users: 32 (over z, x, core), items: 4 (over y).
Axes of the slice: x: 4, y: 4, z: 4, core: 2. Of those that a mesh axis runs over, the one named last changes fastest.
Arguments:
- user_factors: bfloat16 [65536, 256], P('users'), may hold values from -1.5 to 1.5
- item_factors: bfloat16 [4, 4096, 256], P('items', 'users'), may hold values from -1.5 to 1.5
- confidence: bfloat16 [32, 4, 256, 128, 128], P('users', 'items'), may hold values from 0.099609375 to 10
- tile_counts: int32 [32, 4, 256], P('users', 'items'), may hold values from 1 to 4095
- tile_user: int32 [32, 4, 256], P('users', 'items'), may hold values from 0 to 15
- tile_item: int32 [32, 4, 256], P('users', 'items'), may hold values from 0 to 31
- block_slot: int32 [4, 32], P('items'), may hold values from 0 to 31, each once within a row
- live_tiles: int32 [32, 4], P('users', 'items'), may hold values from 64 to 256, as said below
Outputs:
- user_grad: float32 [65536, 256], P('users')
- item_grad: float32 [4, 4096, 256], P('items', 'users')
Inputs may be any that keep to these rules, and one draw needn't show every extreme that they name: Tile slots at positions from live_tiles on are ignored; some user shard and group uses all 256 slots.
All inputs are finite; a program needn't handle non-finite values.
Results may differ from a plain program's by a relative error of at most 0.0012.
Values may be sent and summed in bfloat16 or wider, within the bound.
No kernel may reach another device: no remote copies, remote signals or barrier semaphores. Data moves between devices by JAX's collectives and lax.ppermute only.
A program may use at most 128 MiB of HBM per device.

v0:
```python
import math

import jax
import jax.numpy as jnp
from jax import lax
from jax.sharding import PartitionSpec as P

grad_scale = 0.005
gram_weight = 0.5


def gramian(factor_rows):
    return lax.dot_general(
        factor_rows, factor_rows, (((0,), (0,)), ((), ())), preferred_element_type=jnp.float32
    )


def local(
    user_factors,
    item_factors,
    confidence,
    tile_counts,
    tile_user,
    tile_item,
    block_slot,
    live_tiles,
):
    row_count, rank_size = user_factors.shape
    tile_edge = confidence.shape[3]
    user_block_count = row_count // tile_edge
    user_blocks = user_factors.reshape(user_block_count, tile_edge, rank_size)
    gathered = lax.all_gather(item_factors, "users", axis=1, tiled=True)[0]
    panel_count = gathered.shape[0] // tile_edge
    item_blocks = gathered.reshape(panel_count, tile_edge, rank_size)
    confidence_tiles = confidence[0, 0]
    user_list = tile_user[0, 0]
    slot_list = block_slot[0][tile_item[0, 0]]
    tile_scale = jnp.log1p(tile_counts[0, 0].astype(jnp.float32))
    live_count = live_tiles[0, 0]
    tile_total = confidence_tiles.shape[0]
    step_tiles = math.gcd(tile_total, 32)
    user_ids = jnp.arange(user_block_count, dtype=jnp.int32)
    panel_ids = jnp.arange(panel_count, dtype=jnp.int32)

    def visit_block(block_number, state_pair):
        user_acc, item_acc = state_pair
        first_tile = block_number * step_tiles
        conf_block = lax.dynamic_slice_in_dim(confidence_tiles, first_tile, step_tiles, 0)
        user_pick = lax.dynamic_slice_in_dim(user_list, first_tile, step_tiles, 0)
        slot_pick = lax.dynamic_slice_in_dim(slot_list, first_tile, step_tiles, 0)
        scale_pick = lax.dynamic_slice_in_dim(tile_scale, first_tile, step_tiles, 0)
        live_mask = (first_tile + jnp.arange(step_tiles, dtype=jnp.int32) < live_count).astype(
            jnp.float32
        )
        user_hot = user_pick[:, None] == user_ids[None, :]
        panel_hot = slot_pick[:, None] == panel_ids[None, :]
        user_tiles = jnp.einsum(
            "tu,uak->tak",
            user_hot.astype(jnp.bfloat16),
            user_blocks,
            preferred_element_type=jnp.float32,
        ).astype(jnp.bfloat16)
        item_tiles = jnp.einsum(
            "tp,pak->tak",
            panel_hot.astype(jnp.bfloat16),
            item_blocks,
            preferred_element_type=jnp.float32,
        ).astype(jnp.bfloat16)
        scores = jnp.einsum(
            "tak,tbk->tab", user_tiles, item_tiles, preferred_element_type=jnp.float32
        )
        factor = (scale_pick * live_mask)[:, None, None]
        weighted = (conf_block.astype(jnp.float32) * factor * (scores - 1.0)).astype(jnp.bfloat16)
        user_terms = jnp.einsum(
            "tab,tbk->tak", weighted, item_tiles, preferred_element_type=jnp.float32
        )
        item_terms = jnp.einsum(
            "tab,tak->tbk", weighted, user_tiles, preferred_element_type=jnp.float32
        )
        user_acc = user_acc + jnp.einsum(
            "tu,tak->uak", user_hot.astype(jnp.float32), user_terms, precision=lax.Precision.HIGHEST
        )
        item_acc = item_acc + jnp.einsum(
            "tp,tak->pak",
            panel_hot.astype(jnp.float32),
            item_terms,
            precision=lax.Precision.HIGHEST,
        )
        return (user_acc, item_acc)

    start_pair = (
        jnp.zeros((user_block_count, tile_edge, rank_size), jnp.float32),
        jnp.zeros((panel_count, tile_edge, rank_size), jnp.float32),
    )
    user_acc, item_acc = lax.fori_loop(0, tile_total // step_tiles, visit_block, start_pair)
    user_part = grad_scale * user_acc.reshape(row_count, rank_size)
    item_part = grad_scale * item_acc.reshape(panel_count * tile_edge, rank_size)
    own_panels = item_factors[0]
    user_wide = user_factors.astype(jnp.float32)
    own_wide = own_panels.astype(jnp.float32)
    item_gram = lax.psum(gramian(own_panels), ("users", "items"))
    user_total = lax.psum(user_part, "items")
    user_grad = user_total + grad_scale * gram_weight * jnp.dot(
        user_wide, item_gram, precision=lax.Precision.HIGHEST
    )
    item_total = lax.psum_scatter(item_part, "users", scatter_dimension=0, tiled=True)
    user_gram = lax.psum(gramian(user_factors).astype(jnp.bfloat16), "users").astype(jnp.float32)
    item_grad = item_total + grad_scale * gram_weight * jnp.dot(
        own_wide, user_gram, precision=lax.Precision.HIGHEST
    )
    return (user_grad, item_grad[None])


def solution(mesh):
    in_specs = (
        P("users", None),
        P("items", "users", None),
        P("users", "items", None, None, None),
        P("users", "items", None),
        P("users", "items", None),
        P("users", "items", None),
        P("items", None),
        P("users", "items"),
    )
    out_specs = (P("users", None), P("items", "users", None))
    return jax.shard_map(local, mesh=mesh, in_specs=in_specs, out_specs=out_specs, check_vma=False)
```

profile of v0, /device:TPU:0, one launch (start us, length us, event | category | flops | bytes accessed | tf_op | source)
XLA Modules:
  0.0 557.9 jit_solution(8416958373465999257)
XLA Ops:
  17.1 4.3 compare_select_fusion.2
  21.6 15.7 %select_select_fusion = s32[256]{0:T(256)S(1)} fusion(pred[256]{0:T(512)(128)(4,1)S(1)} %get-tuple-element.366, pred[256]{0:T(512)(128)(4,1)S(1)} %get-tuple-element.365, pred[256]{0:T(512)(128)(4,1)S(1)} %get-tuple-element.364, pred[256]{0:T(512)(128)(4,1)S(1)} %get-tuple-element.363, pred[256]{0:T(512)(128)(4,1)S(1)} %get-tuple-element.362, ...), kind=kLoop, calls=%fused_computation.84 | loop fusion | flops 6400 | bytes 8548 | tf_op jit(solution)/shard_map/gather | solution.py:37
  37.3 20.1 %all-gather.2.cloned.1.call-done = bf16[1,4096,256]{2,1,0:T(8,128)(2,1)} async-done(((bf16[1,128,256]{2,1,0:T(8,128)(2,1)}), bf16[1,4096,256]{2,1,0:T(8,128)(2,1)}) %all-gather.2.cloned.1.call-update) | async-done | bytes 2097168 | tf_op jit(solution)/shard_map/all_gather | solution.py:32
  57.4 2.8 copy.21
  60.2 232.7 %while.18 = (s32[]{:T(128)}, f32[16,128,256]{2,0,1:T(8,128)}, f32[32,128,256]{2,0,1:T(8,128)}, s32[256]{0:T(256)S(1)}, bf16[256,128,128]{2,1,0:T(8,128)(2,1)}, /...) while((s32[]{:T(128)}, f32[16,128,256]{2,0,1:T(8,128)}, ...), condition=%wide.region_1.0_spmd.clone, body=%wide.region_0.0_spmd.clone.sunk | while | flops 1520438400 | bytes 120588176 | solution.py:95
  62.6 2.4 fusion.83
  65.7 4.8 fusion.84
  70.5 7.4 %select_add_fusion.4 = f32[16,128,256]{2,0,1:T(8,128)} fusion(f32[16,128,256]{2,0,1:T(8,128)} %get-tuple-element.497, f32[32,128,256]{2,1,0:T(8,128)} %fusion.84, pred[]{:T(512)S(6)} %compare.128, s32[32]{0:T(128)S(1)} %dynamic_slice.62), kind=kOutput, calls=%fused_computation.7.clone.1 | convolution fusion | flops 202375680 | bytes 8388737 | tf_op jit(solution)/shard_map/while/body/eval_jaxpr/tu,tak->uak/dot_general | solution.py:80
  77.9 3.8 fusion.85
  81.7 5.2 select_add_fusion.5
  91.1 2.4 fusion.83
  94.2 4.8 fusion.84
  99.0 8.1 %select_add_fusion.4 = f32[16,128,256]{2,0,1:T(8,128)} fusion(f32[16,128,256]{2,0,1:T(8,128)} %get-tuple-element.497, f32[32,128,256]{2,1,0:T(8,128)} %fusion.84, pred[]{:T(512)S(6)} %compare.128, s32[32]{0:T(128)S(1)} %dynamic_slice.62), kind=kOutput, calls=%fused_computation.7.clone.1 | convolution fusion | flops 202375680 | bytes 8388737 | tf_op jit(solution)/shard_map/while/body/eval_jaxpr/tu,tak->uak/dot_general | solution.py:80
  107.1 3.8 fusion.85
  110.9 5.2 select_add_fusion.5
  120.3 2.4 fusion.83
  123.4 4.8 fusion.84
  128.1 8.1 %select_add_fusion.4 = f32[16,128,256]{2,0,1:T(8,128)} fusion(f32[16,128,256]{2,0,1:T(8,128)} %get-tuple-element.497, f32[32,128,256]{2,1,0:T(8,128)} %fusion.84, pred[]{:T(512)S(6)} %compare.128, s32[32]{0:T(128)S(1)} %dynamic_slice.62), kind=kOutput, calls=%fused_computation.7.clone.1 | convolution fusion | flops 202375680 | bytes 8388737 | tf_op jit(solution)/shard_map/while/body/eval_jaxpr/tu,tak->uak/dot_general | solution.py:80
  136.2 3.8 fusion.85
  140.0 5.2 select_add_fusion.5
  152.5 4.8 fusion.84
  157.3 8.1 %select_add_fusion.4 = f32[16,128,256]{2,0,1:T(8,128)} fusion(f32[16,128,256]{2,0,1:T(8,128)} %get-tuple-element.497, f32[32,128,256]{2,1,0:T(8,128)} %fusion.84, pred[]{:T(512)S(6)} %compare.128, s32[32]{0:T(128)S(1)} %dynamic_slice.62), kind=kOutput, calls=%fused_computation.7.clone.1 | convolution fusion | flops 202375680 | bytes 8388737 | tf_op jit(solution)/shard_map/while/body/eval_jaxpr/tu,tak->uak/dot_general | solution.py:80
  165.4 3.8 fusion.85
  169.2 5.2 select_add_fusion.5
  181.7 4.8 fusion.84
  186.4 8.1 %select_add_fusion.4 = f32[16,128,256]{2,0,1:T(8,128)} fusion(f32[16,128,256]{2,0,1:T(8,128)} %get-tuple-element.497, f32[32,128,256]{2,1,0:T(8,128)} %fusion.84, pred[]{:T(512)S(6)} %compare.128, s32[32]{0:T(128)S(1)} %dynamic_slice.62), kind=kOutput, calls=%fused_computation.7.clone.1 | convolution fusion | flops 202375680 | bytes 8388737 | tf_op jit(solution)/shard_map/while/body/eval_jaxpr/tu,tak->uak/dot_general | solution.py:80
  194.5 3.8 fusion.85
  198.3 5.2 select_add_fusion.5
  210.8 4.8 fusion.84
  215.6 8.1 %select_add_fusion.4 = f32[16,128,256]{2,0,1:T(8,128)} fusion(f32[16,128,256]{2,0,1:T(8,128)} %get-tuple-element.497, f32[32,128,256]{2,1,0:T(8,128)} %fusion.84, pred[]{:T(512)S(6)} %compare.128, s32[32]{0:T(128)S(1)} %dynamic_slice.62), kind=kOutput, calls=%fused_computation.7.clone.1 | convolution fusion | flops 202375680 | bytes 8388737 | tf_op jit(solution)/shard_map/while/body/eval_jaxpr/tu,tak->uak/dot_general | solution.py:80
  223.7 3.8 fusion.85
  227.5 5.2 select_add_fusion.5
  240.0 4.8 fusion.84
  244.7 8.1 %select_add_fusion.4 = f32[16,128,256]{2,0,1:T(8,128)} fusion(f32[16,128,256]{2,0,1:T(8,128)} %get-tuple-element.497, f32[32,128,256]{2,1,0:T(8,128)} %fusion.84, pred[]{:T(512)S(6)} %compare.128, s32[32]{0:T(128)S(1)} %dynamic_slice.62), kind=kOutput, calls=%fused_computation.7.clone.1 | convolution fusion | flops 202375680 | bytes 8388737 | tf_op jit(solution)/shard_map/while/body/eval_jaxpr/tu,tak->uak/dot_general | solution.py:80
  252.8 3.8 fusion.85
  256.6 5.2 select_add_fusion.5
  269.1 4.8 fusion.84
  273.9 8.1 %select_add_fusion.4 = f32[16,128,256]{2,0,1:T(8,128)} fusion(f32[16,128,256]{2,0,1:T(8,128)} %get-tuple-element.497, f32[32,128,256]{2,1,0:T(8,128)} %fusion.84, pred[]{:T(512)S(6)} %compare.128, s32[32]{0:T(128)S(1)} %dynamic_slice.62), kind=kOutput, calls=%fused_computation.7.clone.1 | convolution fusion | flops 202375680 | bytes 8388737 | tf_op jit(solution)/shard_map/while/body/eval_jaxpr/tu,tak->uak/dot_general | solution.py:80
  282.0 3.8 fusion.85
  285.8 5.2 select_add_fusion.5
  297.0 3.8 copy.51
  303.2 5.1 broadcast_multiply_fusion
  308.3 5.9 %copy.23 = f32[32,128,256]{1,0,2:T(8,128)} copy(f32[32,128,256]{2,0,1:T(8,128)} %broadcast_multiply_fusion) | data formatting | bytes 8388608 | tf_op jit(solution)/shard_map/mul | solution.py:97
  314.3 7.9 %copy.50 = f32[32,8,32,128]{3,1,2,0:T(8,128)} copy(f32[32,8,32,128]{3,2,1,0:T(8,128)} %bitcast.100) | data formatting | bytes 8388608
  322.3 36.4 %all-reduce.4.cloned.1.call-done = f32[2048,256]{0,1:T(8,128)} async-done(((f32[2048,256]{0,1:T(8,128)}), f32[2048,256]{0,1:T(8,128)}) %all-reduce.4.cloned.1.call-update) | async-done | bytes 2097168 | tf_op jit(solution)/shard_map/psum | solution.py:102
  358.7 3.5 fusion.40
  364.0 98.7 %all-reduce.8.cloned.1.call-done = bf16[256,256]{1,0:T(8,128)(2,1)} async-done(((bf16[256,256]{1,0:T(8,128)(2,1)}), bf16[256,256]{1,0:T(8,128)(2,1)}) %all-reduce.8.cloned.1.call-update) | async-done | bytes 131088 | tf_op jit(solution)/shard_map/psum | solution.py:107
  462.7 85.6 %reduce-scatter.2.cloned.1.call-done = f32[128,256]{0,1:T(8,128)} async-done(((f32[4096,256]{0,1:T(8,128)}), f32[128,256]{0,1:T(8,128)}) %reduce-scatter.2.cloned.1.call-update) | async-done | bytes 131088 | tf_op jit(solution)/shard_map/reduce_scatter | solution.py:106
  (174 shorter events, 70.3 us)
Async XLA Ops:
  8.0 9.1 %copy-start.8 = (s32[1,1,256]{2,1,0:T(1,128)S(1)}, s32[1,1,256]{2,1,0:T(1,128)}, u32[]{:S(2)}) copy-start(s32[1,1,256]{2,1,0:T(1,128)} %param.15) | copy-start | bytes 3076
  8.0 49.4 %all-gather.2.cloned.1.call-start = ((), (), s32[]{:S(2)}) async-start(), calls=%async_computation.1 | async-start | bytes 2162688 | tf_op jit(solution)/shard_map/all_gather | solution.py:32
  8.7 313.5 %all-reduce.6.cloned.1.call-start = ((), (), s32[]{:S(2)}) async-start(), calls=%async_computation.3 | async-start | bytes 524288 | tf_op jit(solution)/shard_map/psum | solution.py:101
  10.6 348.0 %all-reduce.4.cloned.1.call-start = ((), (), s32[]{:S(2)}) async-start(), calls=%async_computation.2 | async-start | bytes 4194304 | tf_op jit(solution)/shard_map/psum | solution.py:102
  57.4 2.8 copy-start.9
  62.6 2.4 copy-start
  70.5 7.4 %copy-start.1 = (bf16[32,128,256]{2,0,1:T(8,128)(2,1)S(1)}, bf16[32,128,256]{2,0,1:T(8,128)(2,1)}, u32[]{:S(2)}) copy-start(bf16[32,128,256]{2,0,1:T(8,128)(2,1)} %copy-done) | copy-start | bytes 6291460 | tf_op jit(solution)/shard_map/while
  77.9 3.8 copy-start.2
  81.7 7.1 %copy-start.5 = (bf16[32,128,256]{2,0,1:T(8,128)(2,1)S(1)}, bf16[32,128,256]{2,0,1:T(8,128)(2,1)}, u32[]{:S(2)}) copy-start(bf16[32,128,256]{2,0,1:T(8,128)(2,1)} %copy-done.4) | copy-start | bytes 6291460 | tf_op jit(solution)/shard_map/while
  87.0 1.9 copy-start.3
  91.1 2.4 copy-start
  99.0 8.1 %copy-start.1 = (bf16[32,128,256]{2,0,1:T(8,128)(2,1)S(1)}, bf16[32,128,256]{2,0,1:T(8,128)(2,1)}, u32[]{:S(2)}) copy-start(bf16[32,128,256]{2,0,1:T(8,128)(2,1)} %copy-done) | copy-start | bytes 6291460 | tf_op jit(solution)/shard_map/while
  107.1 3.8 copy-start.2
  110.9 7.1 %copy-start.5 = (bf16[32,128,256]{2,0,1:T(8,128)(2,1)S(1)}, bf16[32,128,256]{2,0,1:T(8,128)(2,1)}, u32[]{:S(2)}) copy-start(bf16[32,128,256]{2,0,1:T(8,128)(2,1)} %copy-done.4) | copy-start | bytes 6291460 | tf_op jit(solution)/shard_map/while
  116.1 1.9 copy-start.3
  120.2 2.4 copy-start
  128.1 8.1 %copy-start.1 = (bf16[32,128,256]{2,0,1:T(8,128)(2,1)S(1)}, bf16[32,128,256]{2,0,1:T(8,128)(2,1)}, u32[]{:S(2)}) copy-start(bf16[32,128,256]{2,0,1:T(8,128)(2,1)} %copy-done) | copy-start | bytes 6291460 | tf_op jit(solution)/shard_map/while
  136.2 3.8 copy-start.2
  140.0 7.2 %copy-start.5 = (bf16[32,128,256]{2,0,1:T(8,128)(2,1)S(1)}, bf16[32,128,256]{2,0,1:T(8,128)(2,1)}, u32[]{:S(2)}) copy-start(bf16[32,128,256]{2,0,1:T(8,128)(2,1)} %copy-done.4) | copy-start | bytes 6291460 | tf_op jit(solution)/shard_map/while
  145.3 1.9 copy-start.3
  149.4 2.4 copy-start
  157.3 8.1 %copy-start.1 = (bf16[32,128,256]{2,0,1:T(8,128)(2,1)S(1)}, bf16[32,128,256]{2,0,1:T(8,128)(2,1)}, u32[]{:S(2)}) copy-start(bf16[32,128,256]{2,0,1:T(8,128)(2,1)} %copy-done) | copy-start | bytes 6291460 | tf_op jit(solution)/shard_map/while
  165.4 3.8 copy-start.2
  169.2 7.1 %copy-start.5 = (bf16[32,128,256]{2,0,1:T(8,128)(2,1)S(1)}, bf16[32,128,256]{2,0,1:T(8,128)(2,1)}, u32[]{:S(2)}) copy-start(bf16[32,128,256]{2,0,1:T(8,128)(2,1)} %copy-done.4) | copy-start | bytes 6291460 | tf_op jit(solution)/shard_map/while
  174.4 1.9 copy-start.3
  178.5 2.4 copy-start
  186.4 8.1 %copy-start.1 = (bf16[32,128,256]{2,0,1:T(8,128)(2,1)S(1)}, bf16[32,128,256]{2,0,1:T(8,128)(2,1)}, u32[]{:S(2)}) copy-start(bf16[32,128,256]{2,0,1:T(8,128)(2,1)} %copy-done) | copy-start | bytes 6291460 | tf_op jit(solution)/shard_map/while
  194.5 3.8 copy-start.2
  198.3 7.2 %copy-start.5 = (bf16[32,128,256]{2,0,1:T(8,128)(2,1)S(1)}, bf16[32,128,256]{2,0,1:T(8,128)(2,1)}, u32[]{:S(2)}) copy-start(bf16[32,128,256]{2,0,1:T(8,128)(2,1)} %copy-done.4) | copy-start | bytes 6291460 | tf_op jit(solution)/shard_map/while
  203.5 1.9 copy-start.3
  207.7 2.4 copy-start
  215.6 8.1 %copy-start.1 = (bf16[32,128,256]{2,0,1:T(8,128)(2,1)S(1)}, bf16[32,128,256]{2,0,1:T(8,128)(2,1)}, u32[]{:S(2)}) copy-start(bf16[32,128,256]{2,0,1:T(8,128)(2,1)} %copy-done) | copy-start | bytes 6291460 | tf_op jit(solution)/shard_map/while
  223.7 3.8 copy-start.2
  227.5 7.1 %copy-start.5 = (bf16[32,128,256]{2,0,1:T(8,128)(2,1)S(1)}, bf16[32,128,256]{2,0,1:T(8,128)(2,1)}, u32[]{:S(2)}) copy-start(bf16[32,128,256]{2,0,1:T(8,128)(2,1)} %copy-done.4) | copy-start | bytes 6291460 | tf_op jit(solution)/shard_map/while
  232.7 1.9 copy-start.3
  236.8 2.4 copy-start
  244.7 8.1 %copy-start.1 = (bf16[32,128,256]{2,0,1:T(8,128)(2,1)S(1)}, bf16[32,128,256]{2,0,1:T(8,128)(2,1)}, u32[]{:S(2)}) copy-start(bf16[32,128,256]{2,0,1:T(8,128)(2,1)} %copy-done) | copy-start | bytes 6291460 | tf_op jit(solution)/shard_map/while
  252.8 3.8 copy-start.2
  256.6 7.2 %copy-start.5 = (bf16[32,128,256]{2,0,1:T(8,128)(2,1)S(1)}, bf16[32,128,256]{2,0,1:T(8,128)(2,1)}, u32[]{:S(2)}) copy-start(bf16[32,128,256]{2,0,1:T(8,128)(2,1)} %copy-done.4) | copy-start | bytes 6291460 | tf_op jit(solution)/shard_map/while
  261.8 1.9 copy-start.3
  266.0 2.4 copy-start
  273.9 8.1 %copy-start.1 = (bf16[32,128,256]{2,0,1:T(8,128)(2,1)S(1)}, bf16[32,128,256]{2,0,1:T(8,128)(2,1)}, u32[]{:S(2)}) copy-start(bf16[32,128,256]{2,0,1:T(8,128)(2,1)} %copy-done) | copy-start | bytes 6291460 | tf_op jit(solution)/shard_map/while
  282.0 3.8 copy-start.2
  285.8 7.1 %copy-start.5 = (bf16[32,128,256]{2,0,1:T(8,128)(2,1)S(1)}, bf16[32,128,256]{2,0,1:T(8,128)(2,1)}, u32[]{:S(2)}) copy-start(bf16[32,128,256]{2,0,1:T(8,128)(2,1)} %copy-done.4) | copy-start | bytes 6291460 | tf_op jit(solution)/shard_map/while
  291.0 1.9 copy-start.3
  300.8 161.9 %all-reduce.8.cloned.1.call-start = ((), (), s32[]{:S(2)}) async-start(), calls=%async_computation.5 | async-start | bytes 262144 | tf_op jit(solution)/shard_map/psum | solution.py:107
  303.2 245.1 %reduce-scatter.2.cloned.1.call-start = ((), (), s32[]{:S(2)}) async-start(), calls=%async_computation.4 | async-start | bytes 4325376 | tf_op jit(solution)/shard_map/reduce_scatter | solution.py:106
  362.2 186.1 %copy-start.7 = (bf16[1,128,256]{2,1,0:T(8,128)(2,1)S(1)}, bf16[1,128,256]{2,1,0:T(8,128)(2,1)}, u32[]{:S(2)}) copy-start(bf16[1,128,256]{2,1,0:T(8,128)(2,1)} %param.11) | copy-start | bytes 196612
  (9 other events, 12.4 us)
Sparse Core Ops, SparseCore 0:
  11.1 46.2 all-gather.1
Sparse Core Ops, SparseCore 1:
  14.0 147.1 all-reduce.5
  300.9 57.7 all-reduce.3
  362.3 100.3 all-reduce.7
  466.4 81.9 reduce-scatter.1
where the time goes:
time: 559 us; the launch traced here: 558 us
  waiting for transfers between devices  242 us (43%)
  matrix products  213 us (38%)
  local copies, waits for them, and re-layouts  53.3 us (10%)
  other arithmetic  33.6 us (6%)
  between operations  15.8 us (3%)
    psum x1, waiting for transfers between devices, local(): lax.psum(gramian(user_factors).astype(jnp.bfloat16), 'users')  98.7 us
    reduce_scatter x1, waiting for transfers between devices, local(): lax.psum_scatter(item_part, 'users', scatter_dimension=0, tiled=True)  85.6 us
    dot_general x8, matrix products, visit_block(): jnp.einsum('tu,tak->uak', user_hot.astype(jnp.float32), user_terms, preci...  64 us
    dot_general x8, matrix products, visit_block(): jnp.einsum('tp,tak->pak', panel_hot.astype(jnp.float32), item_terms, prec...  41.6 us
    dot_general x8, matrix products, visit_block(): jnp.einsum('tab,tbk->tak', weighted, item_tiles, preferred_element_type=j...  38.1 us
    psum x1, waiting for transfers between devices, local(): user_total = lax.psum(user_part, 'items')  36.4 us
    dot_general x8, matrix products, visit_block(): jnp.einsum('tab,tak->tbk', weighted, user_tiles, preferred_element_type=j...  30.3 us
    gather x3, other arithmetic, local(): slot_list = block_slot[0][tile_item[0, 0]]  20.1 us
  transfers between devices with their start and end apart: 5, of which 4 were waited for; matrix products, arithmetic and copies ran while one was open for 50% of the time, Pallas kernels for 0%

commit v1 on v0

v1 whole, which is shorter than its diff:
```python
import jax
import jax.numpy as jnp
from jax import lax
from jax.experimental import pallas as pl
from jax.experimental.pallas import tpu as pltpu
from jax.sharding import PartitionSpec as P

GRAD_SCALE = 0.005
GRAM_WEIGHT = 0.5
SLOTS = 8


def dot(a, b, ca, cb):
    return lax.dot_general(a, b, (((ca,), (cb,)), ((), ())), preferred_element_type=jnp.float32)


def plan_kernel(user_ref, item_ref, slot_ref, live_ref, scale_ref, head_ref, pair_ref, tile_ref, panel_ref, factor_ref, place_ref):
    user_total = place_ref.shape[0]
    pair_total = pair_ref.shape[0]
    live = live_ref[0]

    def clear_user(u, carry):
        place_ref[u] = 0
        return carry

    lax.fori_loop(0, user_total, clear_user, 0)

    def clear_pair(p, carry):
        tile_ref[p] = 0
        panel_ref[p] = 0
        factor_ref[p] = 0.0
        return carry

    lax.fori_loop(0, 2 * pair_total, clear_pair, 0)

    def count(t, carry):
        u = user_ref[t]
        place_ref[u] = place_ref[u] + 1
        return carry

    lax.fori_loop(0, live, count, 0)

    def start(u, first):
        pairs = (place_ref[u] + 1) // 2
        place_ref[u] = 2 * first

        def name(p, carry):
            pair_ref[p] = u
            return carry

        lax.fori_loop(first, first + pairs, name, 0)
        return first + pairs

    head_ref[0] = lax.fori_loop(0, user_total, start, 0)

    def put(t, carry):
        u = user_ref[t]
        spot = place_ref[u]
        place_ref[u] = spot + 1
        tile_ref[spot] = t
        panel_ref[spot] = slot_ref[item_ref[t]]
        factor_ref[spot] = scale_ref[t]
        return carry

    lax.fori_loop(0, live, put, 0)


def split(x):
    high = x.astype(jnp.bfloat16)
    return high, (x - high.astype(jnp.float32)).astype(jnp.bfloat16)


def tile_kernel(head_ref, pair_ref, tile_ref, panel_ref, factor_ref, users_ref, items_ref, conf_ref, user_out, item_out, conf_buf, sems):
    edge = conf_buf.shape[2]
    pairs = head_ref[0]

    def copies(p, slot):
        return [
            pltpu.make_async_copy(conf_ref.at[tile_ref[2 * p + k]], conf_buf.at[slot, k], sems.at[slot, k])
            for k in range(2)
        ]

    def fetch(p, slot):
        for c in copies(p, slot):
            c.start()

    for s in range(SLOTS):
        @pl.when(s < pairs)
        def _():
            fetch(s, s)

    item_gram = dot(items_ref[...], items_ref[...], 0, 0)
    user_gram = dot(users_ref[...], users_ref[...], 0, 0)
    high, low = split(GRAM_WEIGHT * item_gram)
    user_out[...] = dot(users_ref[...], high, 1, 0) + dot(users_ref[...], low, 1, 0)
    high, low = split(GRAM_WEIGHT * user_gram)
    item_out[...] = dot(items_ref[...], high, 1, 0) + dot(items_ref[...], low, 1, 0)

    def visit(p, carry):
        slot = lax.rem(p, SLOTS)
        u = pl.multiple_of(pair_ref[p] * edge, edge)
        v0 = pl.multiple_of(panel_ref[2 * p] * edge, edge)
        v1 = pl.multiple_of(panel_ref[2 * p + 1] * edge, edge)
        users = users_ref[pl.ds(u, edge), :]
        items = jnp.concatenate([items_ref[pl.ds(v0, edge), :], items_ref[pl.ds(v1, edge), :]], axis=0)
        scores = dot(users, items, 1, 1)
        for c in copies(p, slot):
            c.wait()
        left = conf_buf[slot, 0].astype(jnp.float32) * factor_ref[2 * p] * (scores[:, :edge] - 1.0)
        right = conf_buf[slot, 1].astype(jnp.float32) * factor_ref[2 * p + 1] * (scores[:, edge:] - 1.0)

        @pl.when(p + SLOTS < pairs)
        def _():
            fetch(p + SLOTS, slot)

        weighted = jnp.concatenate([left, right], axis=1).astype(jnp.bfloat16)
        user_out[pl.ds(u, edge), :] += dot(weighted, items, 1, 0)
        item_terms = dot(weighted, users, 0, 0)
        item_out[pl.ds(v0, edge), :] += item_terms[:edge]
        item_out[pl.ds(v1, edge), :] += item_terms[edge:]
        return carry

    lax.fori_loop(0, pairs, visit, 0)


def smem():
    return pl.BlockSpec(memory_space=pltpu.SMEM)


def vmem():
    return pl.BlockSpec(memory_space=pltpu.VMEM)


def local(user_factors, item_factors, confidence, tile_counts, tile_user, tile_item, block_slot, live_tiles):
    rows, rank = user_factors.shape
    tiles, edge = confidence.shape[2:4]
    blocks = rows // edge
    pairs = (tiles + blocks) // 2
    scale = jnp.log1p(tile_counts[0, 0].astype(jnp.float32))
    i32 = jnp.int32
    plan = pl.pallas_call(
        plan_kernel,
        out_shape=(
            jax.ShapeDtypeStruct((1,), i32),
            jax.ShapeDtypeStruct((pairs,), i32),
            jax.ShapeDtypeStruct((2 * pairs,), i32),
            jax.ShapeDtypeStruct((2 * pairs,), i32),
            jax.ShapeDtypeStruct((2 * pairs,), jnp.float32),
        ),
        in_specs=[smem()] * 5,
        out_specs=[smem()] * 5,
        scratch_shapes=[pltpu.SMEM((blocks,), i32)],
        name="plan",
    )(tile_user[0, 0], tile_item[0, 0], block_slot[0], live_tiles[0], scale)
    items = lax.all_gather(item_factors, "users", axis=1, tiled=True)[0]
    user_part, item_part = pl.pallas_call(
        tile_kernel,
        out_shape=(
            jax.ShapeDtypeStruct((rows, rank), jnp.float32),
            jax.ShapeDtypeStruct(items.shape, jnp.float32),
        ),
        in_specs=[smem()] * 5 + [vmem(), vmem(), pl.BlockSpec(memory_space=pl.ANY)],
        out_specs=[vmem(), vmem()],
        scratch_shapes=[pltpu.VMEM((SLOTS, 2, edge, edge), jnp.bfloat16), pltpu.SemaphoreType.DMA((SLOTS, 2))],
        name="tiles",
    )(*plan, user_factors, items, confidence[0, 0])
    user_grad = GRAD_SCALE * lax.psum(user_part, "items")
    item_grad = GRAD_SCALE * lax.psum_scatter(item_part, "users", scatter_dimension=0, tiled=True)
    return user_grad, item_grad[None]


def solution(mesh):
    in_specs = (
        P("users", None),
        P("items", "users", None),
        P("users", "items", None, None, None),
        P("users", "items", None),
        P("users", "items", None),
        P("users", "items", None),
        P("items", None),
        P("users", "items"),
    )
    out_specs = (P("users", None), P("items", "users", None))
    return jax.shard_map(local, mesh=mesh, in_specs=in_specs, out_specs=out_specs, check_vma=False)
```

time: 559 us -> 276 us (0.49)
  matrix products: 213 us -> 0 us
  local copies, waits for them, and re-layouts: 53.3 us -> 0 us
  Pallas kernels: 0 us -> 36.9 us
  other arithmetic: 33.6 us -> 5.91 us
  waiting for transfers between devices: 242 us -> 219 us
    dot_general x60 -> x0, matrix products: 213 us -> none  [the longest x8 64 us: visit_block(): jnp.einsum('tu,tak->uak', user_hot.astype(jnp.float32), user_terms, preci...]
    psum x3 -> x1, waiting for transfers between devices: 135 us -> 94.1 us  [local(): user_grad = GRAD_SCALE * lax.psum(user_part, 'items')]
    pallas_call x0 -> x2, Pallas kernels: none -> 36.9 us  [the longest x1 31.1 us: local(): pl.pallas_call(tile_kernel, out_shape=(jax.ShapeDtypeStruct((rows, rank),...]
    all_gather x1, waiting for transfers between devices: 20.1 us -> 40.8 us  [local(): items = lax.all_gather(item_factors, 'users', axis=1, tiled=True)[0]]
    gather x3 -> x0, other arithmetic: 20.1 us -> none  [local(): slot_list = block_slot[0][tile_item[0, 0]]]
    unnamed x14 -> x0, local copies, waits for them, and re-layouts: 20.1 us -> none
    while x96 -> x0, local copies, waits for them, and re-layouts: 20 us -> none
    mul x10 -> x1, other arithmetic: 12.8 us -> 3.09 us  [local(): user_grad = GRAD_SCALE * lax.psum(user_part, 'items')]
  transfers between devices with their start and end apart: 5 -> 3, of which waited for: 4 -> 3; matrix products, arithmetic and copies ran while one was open for 50% -> 2% of each run, Pallas kernels for 0% -> 2%
where the time goes in v1:
time: 276 us
  waiting for transfers between devices  219 us (79%)
  Pallas kernels  36.9 us (13%)
  between operations  14.4 us (5%)
  other arithmetic  5.91 us (2%)
    psum x1, waiting for transfers between devices, local(): user_grad = GRAD_SCALE * lax.psum(user_part, 'items')  94.1 us
    reduce_scatter x1, waiting for transfers between devices, local(): lax.psum_scatter(item_part, 'users', scatter_dimension=0, tiled=True)  82.8 us
    all_gather x1, waiting for transfers between devices, local(): items = lax.all_gather(item_factors, 'users', axis=1, tiled=True)[0]  40.8 us
    pallas_call x1, Pallas kernels, local(): pl.pallas_call(tile_kernel, out_shape=(jax.ShapeDtypeStruct((rows, rank),...  31.1 us
    pallas_call x1, Pallas kernels, local(): pl.pallas_call(plan_kernel, out_shape=(jax.ShapeDtypeStruct((1,), i32), j...  5.79 us
  transfers between devices with their start and end apart: 3, of which 3 were waited for; matrix products, arithmetic and copies ran while one was open for 2% of the time, Pallas kernels for 2%

profile of v1, /device:TPU:0, one launch (start us, length us, event | category | flops | bytes accessed | tf_op | source)
XLA Modules:
  0.0 276.5 jit_solution(3858818877626222012)
XLA Ops:
  7.2 0.0 all-gather.2.cloned.1.call-start
  7.2 0.7 all-gather.2.cloned.1.call-update
  7.9 0.0 all-reduce.2.cloned.1.call-start
  8.6 1.3 convert_log-plus-one_fusion
  9.8 5.8 %plan.1 = (s32[1]{0:T(128)}, s32[136]{0:T(256)}, s32[272]{0:T(512)}, s32[272]{0:T(512)}, f32[272]{0:T(512)}) custom-call(s32[256]{0:T(256)} %bitcast.13, s32[256]{0:T(256)} %bitcast.14, s32[32]{0:T(128)} %bitcast.15, s32[1]{0:T(128)} %bitcast.9.live_ref, f32[256]{0:T(256)} %bitcast.12), custom_call_target="tpu_custom_call" | custom-call | tf_op jit(solution)/shard_map/plan/pallas_call | solution.py:141
  15.6 40.8 %all-gather.2.cloned.1.call-done = bf16[1,4096,256]{2,1,0:T(8,128)(2,1)} async-done(((bf16[1,128,256]{2,1,0:T(8,128)(2,1)}), bf16[1,4096,256]{2,1,0:T(8,128)(2,1)}) %all-gather.2.cloned.1.call-update) | async-done | bytes 2097168 | tf_op jit(solution)/shard_map/all_gather | solution.py:155
  56.5 31.1 %tiles.1 = (f32[2048,256]{1,0:T(8,128)}, f32[4096,256]{1,0:T(8,128)}) custom-call(s32[1]{0:T(128)} %get-tuple-element.9.head_ref, s32[136]{0:T(256)} %get-tuple-element.10.pair_ref, s32[272]{0:T(512)} %get-tuple-element.11.tile_ref, s32[272]{0:T(512)} %get-tuple-element.12.panel_ref, f32[272]{0:T(512)} %get-tuple-element.13.factor_ref, ...), custom_call_target="tpu_custom_call" | custom-call | tf_op jit(solution)/shard_map/tiles/pallas_call | solution.py:156
  87.6 0.0 all-reduce.2.cloned.1.call-update
  87.6 0.0 reduce-scatter.2.cloned.1.call-start
  87.6 0.7 reduce-scatter.2.cloned.1.call-update
  88.3 94.1 %all-reduce.2.cloned.1.call-done = f32[2048,256]{1,0:T(8,128)} async-done(((f32[2048,256]{1,0:T(8,128)}), f32[2048,256]{1,0:T(8,128)}) %all-reduce.2.cloned.1.call-update) | async-done | bytes 2097168 | tf_op jit(solution)/shard_map/psum | solution.py:167
  182.4 3.1 %broadcast_multiply_fusion = f32[2048,256]{1,0:T(8,128)} fusion(f32[2048,256]{1,0:T(8,128)} %all-reduce.2.cloned.1.call-done), kind=kLoop, calls=%fused_computation | loop fusion | flops 524288 | bytes 4194304 | tf_op jit(solution)/shard_map/mul | solution.py:167
  185.5 82.8 %reduce-scatter.2.cloned.1.call-done = f32[128,256]{1,0:T(8,128)} async-done(((f32[4096,256]{1,0:T(8,128)}), f32[128,256]{1,0:T(8,128)}) %reduce-scatter.2.cloned.1.call-update) | async-done | bytes 131088 | tf_op jit(solution)/shard_map/reduce_scatter | solution.py:168
  268.4 1.6 multiply_bitcast_fusion
Async XLA Ops:
  7.2 49.3 %all-gather.2.cloned.1.call-start = ((), (), s32[]{:S(2)}) async-start(), calls=%async_computation.1 | async-start | bytes 2162688 | tf_op jit(solution)/shard_map/all_gather | solution.py:155
  7.9 174.5 %all-reduce.2.cloned.1.call-start = ((), (), s32[]{:S(2)}) async-start(), calls=%async_computation.2 | async-start | bytes 4194304 | tf_op jit(solution)/shard_map/psum | solution.py:167
  87.6 180.8 %reduce-scatter.2.cloned.1.call-start = ((), (), s32[]{:S(2)}) async-start(), calls=%async_computation.3 | async-start | bytes 4325376 | tf_op jit(solution)/shard_map/reduce_scatter | solution.py:168
Sparse Core Ops, SparseCore 0:
  10.2 46.1 all-gather.1
  87.7 94.6 all-reduce.1
  186.1 82.2 reduce-scatter.1
